TPU v7x, 32 devices: a whole 2x2x4 slice. The times are simulated.
32 devices in a mesh: dp: 8 (over z, y), ctx: 4 (over x, core).
Axes of the slice: x: 2, y: 2, z: 4, core: 2. Of those that a mesh axis runs over, the one named last changes fastest.
Arguments:
- projected: bfloat16 [8, 512, 3, 4096], P('dp', 'ctx'), may hold values from -6 to 6
- short_taps: float32 [3, 3, 4096], P(None, None, 'ctx'), may hold values from -3 to 3
- long_filter: bfloat16 [512, 4096], P('dp', 'ctx'), may hold values from -1.1 to 1.1
- skip_gain: float32 [4096], P('ctx'), may hold values from -4 to 4
Outputs:
- mixed: bfloat16 [8, 512, 4096], P('dp', 'ctx')
All inputs are finite; a program needn't handle non-finite values.
Results may differ from a plain program's by a relative error of at most 0.012.
Values may be sent and summed in bfloat16 or wider, within the bound.
A program may use at most 64 MiB of HBM per device.

v0:
```python
import math
import jax
import jax.numpy as jnp
from jax import lax
from jax.sharding import PartitionSpec as P

RADIX = 64
HIGH = lax.Precision.HIGHEST


def causal_short(extended, taps, kernel_size):
    row_count = extended.shape[0] - (kernel_size - 1)
    widened = extended.astype(jnp.float32)
    summed = jnp.zeros((row_count,) + widened.shape[1:], jnp.float32)
    for tap_index in range(kernel_size):
        offset = kernel_size - 1 - tap_index
        summed = summed + taps[tap_index] * widened[offset : offset + row_count]
    return (summed[:, 0].astype(jnp.bfloat16), (summed[:, 1] * summed[:, 2]).astype(jnp.bfloat16))


def dft_tables(length, radix_size):
    outer_size = 2 * length // radix_size
    total_size = outer_size * radix_size
    outer_range = jnp.arange(outer_size, dtype=jnp.int32)
    inner_range = jnp.arange(radix_size, dtype=jnp.int32)
    angle_one = (
        2.0
        * math.pi
        / outer_size
        * (outer_range[:, None] * outer_range[None, :] % outer_size).astype(jnp.float32)
    )
    angle_twist = (
        2.0
        * math.pi
        / total_size
        * (outer_range[:, None] * inner_range[None, :] % total_size).astype(jnp.float32)
    )
    angle_two = (
        2.0
        * math.pi
        / radix_size
        * (inner_range[:, None] * inner_range[None, :] % radix_size).astype(jnp.float32)
    )
    twist_cos = jnp.cos(angle_twist)[:, :, None]
    twist_sin = jnp.sin(angle_twist)[:, :, None]
    return (
        jnp.cos(angle_one),
        jnp.sin(angle_one),
        twist_cos,
        twist_sin,
        jnp.cos(angle_two),
        jnp.sin(angle_two),
    )


def forward_dft(signal, tables, radix_size):
    cos_one, sin_one, twist_cos, twist_sin, cos_two, sin_two = tables
    outer_size = cos_one.shape[0]
    half_size = outer_size // 2
    block_width = signal.shape[1]
    shaped = signal.reshape(half_size, radix_size * block_width)
    first_re = jnp.dot(cos_one[:, :half_size], shaped, precision=HIGH).reshape(
        outer_size, radix_size, block_width
    )
    first_im = -jnp.dot(sin_one[:, :half_size], shaped, precision=HIGH).reshape(
        outer_size, radix_size, block_width
    )
    second_re = first_re * twist_cos + first_im * twist_sin
    second_im = first_im * twist_cos - first_re * twist_sin
    spec_re = jnp.einsum("amc,mb->abc", second_re, cos_two, precision=HIGH) + jnp.einsum(
        "amc,mb->abc", second_im, sin_two, precision=HIGH
    )
    spec_im = jnp.einsum("amc,mb->abc", second_im, cos_two, precision=HIGH) - jnp.einsum(
        "amc,mb->abc", second_re, sin_two, precision=HIGH
    )
    return (spec_re, spec_im)


def inverse_dft(spec_re, spec_im, tables, radix_size):
    cos_one, sin_one, twist_cos, twist_sin, cos_two, sin_two = tables
    outer_size = cos_one.shape[0]
    half_size = outer_size // 2
    block_width = spec_re.shape[2]
    back_re = jnp.einsum("abc,mb->amc", spec_re, cos_two, precision=HIGH) - jnp.einsum(
        "abc,mb->amc", spec_im, sin_two, precision=HIGH
    )
    back_im = jnp.einsum("abc,mb->amc", spec_re, sin_two, precision=HIGH) + jnp.einsum(
        "abc,mb->amc", spec_im, cos_two, precision=HIGH
    )
    turned_re = (back_re * twist_cos - back_im * twist_sin).reshape(
        outer_size, radix_size * block_width
    )
    turned_im = (back_re * twist_sin + back_im * twist_cos).reshape(
        outer_size, radix_size * block_width
    )
    result = jnp.dot(cos_one[:half_size], turned_re, precision=HIGH) - jnp.dot(
        sin_one[:half_size], turned_im, precision=HIGH
    )
    return result.reshape(half_size * radix_size, block_width) / (outer_size * radix_size)


def long_convolve(gated_slab, filter_slab):
    length, channels = gated_slab.shape
    block_width = min(128, channels)
    tables = dft_tables(length, RADIX)

    def one_block(block_index, output):
        offset = block_index * block_width
        signal = lax.dynamic_slice_in_dim(gated_slab, offset, block_width, 1).astype(jnp.float32)
        kernel_block = lax.dynamic_slice_in_dim(filter_slab, offset, block_width, 1).astype(
            jnp.float32
        )
        sig_re, sig_im = forward_dft(signal, tables, RADIX)
        ker_re, ker_im = forward_dft(kernel_block, tables, RADIX)
        prod_re = sig_re * ker_re - sig_im * ker_im
        prod_im = sig_re * ker_im + sig_im * ker_re
        result = inverse_dft(prod_re, prod_im, tables, RADIX)
        return lax.dynamic_update_slice_in_dim(output, result, offset, 1)

    return lax.fori_loop(
        0, channels // block_width, one_block, jnp.zeros((length, channels), jnp.float32)
    )


def make_response(gated_slab, filter_slab, skip_gain):
    long_part = long_convolve(gated_slab, filter_slab)
    return (long_part + skip_gain * gated_slab.astype(jnp.float32)).astype(jnp.bfloat16)


def combine_rows(query_part, response_part):
    return (query_part.astype(jnp.float32) * response_part.astype(jnp.float32)).astype(jnp.bfloat16)


def on_device(projected, short_taps, long_filter, skip_gain):
    kernel_size = short_taps.shape[0]
    tok_rows = projected[0]
    filter_slab = lax.all_gather(long_filter, "dp", axis=0, tiled=True)
    stream_slab = lax.all_to_all(tok_rows, "ctx", split_axis=2, concat_axis=0, tiled=True)
    extended = jnp.pad(stream_slab, ((kernel_size - 1, 0), (0, 0), (0, 0)))
    query_slab, gated_slab = causal_short(extended, short_taps, kernel_size)
    response_slab = make_response(gated_slab, filter_slab, skip_gain)
    mixed = lax.all_to_all(
        combine_rows(query_slab, response_slab), "ctx", split_axis=0, concat_axis=1, tiled=True
    )
    return mixed[None]


def solution(mesh):
    return jax.shard_map(
        on_device,
        mesh=mesh,
        in_specs=(P("dp", "ctx", None, None), P(None, None, "ctx"), P("dp", "ctx"), P("ctx")),
        out_specs=P("dp", "ctx", None),
        check_vma=False,
    )
```

profile of v0, /device:TPU:0, one launch (start us, length us, event | category | flops | bytes accessed | tf_op | source)
XLA Modules:
  0.0 225.1 jit_solution(1443863807638157853)
XLA Ops:
  6.5 7.2 %copy.33 = bf16[1,128,3,4096]{1,2,3,0:T(4,128)(2,1)} copy(bf16[1,128,3,4096]{3,1,2,0:T(8,128)(2,1)} %param.6) | data formatting | bytes 6291456 | tf_op args[0]
  13.8 5.0 %all-to-all-start = ((bf16[128,3,4096]{0,1,2:T(4,128)(2,1)}), bf16[128,3,4096]{0,1,2:T(4,128)(2,1)}, u32[]{:S(2)}, u32[]{:S(2)}) async-start(bf16[128,3,4096]{0,1,2:T(4,128)(2,1)} %bitcast.224), calls=%async_computation | async-start | bytes 8388608 | tf_op jit(solution)/shard_map/all_to_all | solution.py:138
  19.6 48.0 %all-to-all-done = bf16[128,3,4096]{0,1,2:T(4,128)(2,1)} async-done(((bf16[128,3,4096]{0,1,2:T(4,128)(2,1)}), bf16[128,3,4096]{0,1,2:T(4,128)(2,1)}, u32[]{:S(2)}, u32[]{:S(2)}) %all-to-all-start) | async-done | bytes 3145760 | tf_op jit(solution)/shard_map/all_to_all | solution.py:138
  67.6 5.5 %copy.34 = bf16[4,128,3,1024]{3,1,0,2:T(8,128)(2,1)S(1)} copy(bf16[4,128,3,1024]{1,2,3,0:T(4,128)(2,1)} %bitcast.3) | data formatting | bytes 6291456 | tf_op jit(solution)/shard_map/all_to_all | solution.py:138
  73.1 0.9 pad_convert_fusion
  74.0 1.9 fusion.123
  75.9 2.6 %copy-done = f32[512,3,1024]{2,0,1:T(8,128)} copy-done((f32[512,3,1024]{2,0,1:T(8,128)}, f32[512,3,1024]{2,0,1:T(8,128)S(1)}, u32[]{:S(2)}) %copy-start) | copy-done | bytes 6291480
  78.6 1.3 fusion.128
  80.1 115.5 %while.15 = (s32[]{:T(128)}, f32[512,1024]{1,0:T(8,128)S(1)}, bf16[512,1024]{1,0:T(8,128)(2,1)}, f32[16,16]{1,0:T(8,128)S(1)}, f32[16,16]{1,0:T(8,128)S(1)}, /*i...) while((s32[]{:T(128)}, f32[512,1024]{1,0:T(8,128)S(1)}, ...), condition=%wide.region_1.2_spmd.clone.clone, body=%wide.region_0.1_spmd.clone.clone.sunk | while | flops 1288484864 | bytes 33853592 | solution.py:120
  80.3 1.0 constant_dynamic-slice_fusion.3
  84.6 0.8 convolution_subtract_fusion.6
  89.2 0.9 multiply_add_fusion.4
  92.3 0.9 multiply_add_fusion.5
  94.7 1.0 constant_dynamic-slice_fusion.3
  99.0 0.8 convolution_subtract_fusion.6
  102.1 0.8 convolution_add_fusion.5
  103.6 0.9 multiply_add_fusion.4
  106.7 0.9 multiply_add_fusion.5
  109.1 1.0 constant_dynamic-slice_fusion.3
  113.4 0.8 convolution_subtract_fusion.6
  116.5 0.8 convolution_add_fusion.5
  118.0 0.9 multiply_add_fusion.4
  121.1 0.9 multiply_add_fusion.5
  123.5 1.0 constant_dynamic-slice_fusion.3
  127.8 0.8 convolution_subtract_fusion.6
  130.9 0.8 convolution_add_fusion.5
  132.4 0.9 multiply_add_fusion.4
  135.5 0.9 multiply_add_fusion.5
  138.0 1.0 constant_dynamic-slice_fusion.3
  142.2 0.8 convolution_subtract_fusion.6
  145.3 0.8 convolution_add_fusion.5
  146.8 0.9 multiply_add_fusion.4
  149.9 0.9 multiply_add_fusion.5
  152.4 1.0 constant_dynamic-slice_fusion.3
  156.6 0.8 convolution_subtract_fusion.6
  161.2 0.9 multiply_add_fusion.4
  164.4 0.9 multiply_add_fusion.5
  166.8 1.0 constant_dynamic-slice_fusion.3
  171.1 0.8 convolution_subtract_fusion.6
  175.6 0.9 multiply_add_fusion.4
  178.8 0.9 multiply_add_fusion.5
  181.2 1.0 constant_dynamic-slice_fusion.3
  185.5 0.8 convolution_subtract_fusion.6
  190.0 0.9 multiply_add_fusion.4
  193.2 0.9 multiply_add_fusion.5
  195.6 3.8 %fusion.126 = bf16[512,1024]{1,0:T(8,128)(2,1)S(1)} fusion(f32[512,1024]{1,0:T(8,128)S(1)} %get-tuple-element.246, f32[512,3,1024]{2,0,1:T(8,128)} %copy-done, f32[1024]{0:T(1024)S(1)} %copy-done.2), kind=kLoop, calls=%fused_computation.151 | loop fusion | flops 5242880 | bytes 8392704 | tf_op jit(solution)/shard_map/convert_element_type | solution.py:131
  199.4 16.9 %all_to_all.34 = bf16[4,128,1024]{2,1,0:T(8,128)(2,1)S(1)} all-to-all(bf16[4,128,1024]{2,1,0:T(8,128)(2,1)S(1)} %bitcast.227), channel_id=1, replica_groups=mesh['dp'=8,'ctx'=4] {'ctx'}, dimensions={0} | all-to-all | bytes 2097152 | tf_op jit(solution)/shard_map/all_to_all | solution.py:142
  217.0 1.3 copy.36
  (208 shorter events, 83.7 us)
Async XLA Ops:
  13.8 5.8 %copy-start.1 = (f32[3,3,1024]{2,1,0:T(4,128)S(1)}, f32[3,3,1024]{2,1,0:T(4,128)}, u32[]{:S(2)}) copy-start(f32[3,3,1024]{2,1,0:T(4,128)} %param.7) | copy-start | bytes 110596
  13.8 53.8 %all-to-all-start = ((bf16[128,3,4096]{0,1,2:T(4,128)(2,1)}), bf16[128,3,4096]{0,1,2:T(4,128)(2,1)}, u32[]{:S(2)}, u32[]{:S(2)}) async-start(bf16[128,3,4096]{0,1,2:T(4,128)(2,1)} %bitcast.224), calls=%async_computation | async-start | bytes 8388608 | tf_op jit(solution)/shard_map/all_to_all | solution.py:138
  18.7 61.1 %all-gather.2.cloned.1.call-start = ((), (), s32[]{:S(2)}) async-start(), calls=%async_computation.2 | async-start | bytes 1179648 | tf_op jit(solution)/shard_map/all_gather | solution.py:137
  75.9 2.7 %copy-start = (f32[512,3,1024]{2,0,1:T(8,128)}, f32[512,3,1024]{2,0,1:T(8,128)S(1)}, u32[]{:S(2)}) copy-start(f32[512,3,1024]{2,0,1:T(8,128)S(1)} %fusion.123) | copy-start | bytes 18874372
  80.1 115.5 %copy-start.2 = (f32[1024]{0:T(1024)S(1)}, f32[1024]{0:T(1024)}, u32[]{:S(2)}) copy-start(f32[1024]{0:T(1024)} %param.9) | copy-start | bytes 12292
Sparse Core Ops, SparseCore 0:
  21.7 43.2 all-gather.1
where the time goes:
time: 226 us; the launch traced here: 225 us
  matrix products  96.6 us (43%)
  waiting for transfers between devices  48.7 us (22%)
  local copies, waits for them, and re-layouts  30.4 us (13%)
  blocking collectives  16.9 us (7%)
  between operations  13.5 us (6%)
  other arithmetic  11.9 us (5%)
  starting transfers between devices  5.02 us (2%)
    all_to_all x1, waiting for transfers between devices, on_device(): lax.all_to_all(tok_rows, 'ctx', split_axis=2, concat_axis=0, tiled=True)  48 us
    all_to_all x1, blocking collectives, on_device(): lax.all_to_all(combine_rows(query_slab, response_slab), 'ctx', split_axis...  16.9 us
    dot_general x16, matrix products, forward_dft(): jnp.einsum('amc,mb->abc', second_re, sin_two, precision=HIGH)  13.3 us
    dot_general x16, matrix products, forward_dft(): jnp.einsum('amc,mb->abc', second_im, sin_two, precision=HIGH)  12.1 us
    dot_general x16, matrix products, forward_dft(): jnp.einsum('amc,mb->abc', second_re, cos_two, precision=HIGH)  12 us
    dot_general x16, matrix products, forward_dft(): jnp.einsum('amc,mb->abc', second_im, cos_two, precision=HIGH)  12 us
    unnamed x7, local copies, waits for them, and re-layouts  9.88 us
    dynamic_slice x8, local copies, waits for them, and re-layouts, one_block(): lax.dynamic_slice_in_dim(filter_slab, offset, block_width, 1)  7.97 us
  transfers between devices with their start and end apart: 2, of which 1 were waited for; matrix products, arithmetic and copies ran while one was open for 4% of the time, Pallas kernels for 0%

commit v1 on v0

--- a/solution.py
+++ b/solution.py
@@ -1,3 +1,4 @@
+import functools
 import math
 import jax
 import jax.numpy as jnp
@@ -6,6 +7,17 @@
 
 RADIX = 64
 HIGH = lax.Precision.HIGHEST
+
+
+def hold_the_shifts_all(state, group_axis):
+    heard = lax.axis_size(group_axis)
+    known = jnp.split(state, heard, axis=2)
+    inter = jnp.stack(known, axis=0)
+    f_now = lax.all_to_all(inter, group_axis, 0, 0)
+    return jnp.concatenate(f_now, axis=0)
+
+
+return_all_the_groups = functools.partial(hold_the_shifts_all, group_axis="ctx")
 
 
 def causal_short(extended, taps, kernel_size):
@@ -135,7 +147,7 @@
     kernel_size = short_taps.shape[0]
     tok_rows = projected[0]
     filter_slab = lax.all_gather(long_filter, "dp", axis=0, tiled=True)
-    stream_slab = lax.all_to_all(tok_rows, "ctx", split_axis=2, concat_axis=0, tiled=True)
+    stream_slab = return_all_the_groups(tok_rows)
     extended = jnp.pad(stream_slab, ((kernel_size - 1, 0), (0, 0), (0, 0)))
     query_slab, gated_slab = causal_short(extended, short_taps, kernel_size)
     response_slab = make_response(gated_slab, filter_slab, skip_gain)

time: 226 us -> 207 us (0.916)
  waiting for transfers between devices: 48.7 us -> 38.5 us
  local copies, waits for them, and re-layouts: 30.4 us -> 20.2 us
    all_to_all x1, waiting for transfers between devices: 48 us -> 36.2 us  [hold_the_shifts_all(): f_now = lax.all_to_all(inter, group_axis, 0, 0)]
    unnamed x7 -> x6, local copies, waits for them, and re-layouts: 9.88 us -> 2.67 us
    all_to_all x1, local copies, waits for them, and re-layouts: 5.51 us -> 0.35 us  [hold_the_shifts_all(): f_now = lax.all_to_all(inter, group_axis, 0, 0)]
  transfers between devices with their start and end apart: 2 -> 2, of which waited for: 1 -> 2; matrix products, arithmetic and copies ran while one was open for 4% -> 2% of each run, Pallas kernels for 0% -> 0%
where the time goes in v1:
time: 207 us; the launch traced here: 206 us
  matrix products  96.6 us (47%)
  waiting for transfers between devices  38.5 us (19%)
  local copies, waits for them, and re-layouts  20.2 us (10%)
  blocking collectives  17 us (8%)
  other arithmetic  13.8 us (7%)
  between operations  13.5 us (7%)
  starting transfers between devices  4.34 us (2%)
    all_to_all x1, waiting for transfers between devices, hold_the_shifts_all(): f_now = lax.all_to_all(inter, group_axis, 0, 0)  36.2 us
    all_to_all x1, blocking collectives, on_device(): lax.all_to_all(combine_rows(query_slab, response_slab), 'ctx', split_axis...  17 us
    dot_general x16, matrix products, forward_dft(): jnp.einsum('amc,mb->abc', second_re, sin_two, precision=HIGH)  13.3 us
    dot_general x16, matrix products, forward_dft(): jnp.einsum('amc,mb->abc', second_im, sin_two, precision=HIGH)  12.1 us
    dot_general x16, matrix products, forward_dft(): jnp.einsum('amc,mb->abc', second_re, cos_two, precision=HIGH)  12 us
    dot_general x16, matrix products, forward_dft(): jnp.einsum('amc,mb->abc', second_im, cos_two, precision=HIGH)  12 us
    dynamic_slice x8, local copies, waits for them, and re-layouts, one_block(): lax.dynamic_slice_in_dim(filter_slab, offset, block_width, 1)  7.97 us
    dot_general x8, matrix products, inverse_dft(): jnp.einsum('abc,mb->amc', spec_im, cos_two, precision=HIGH)  7.17 us
  transfers between devices with their start and end apart: 2, of which 2 were waited for; matrix products, arithmetic and copies ran while one was open for 2% of the time, Pallas kernels for 0%

profile of v1, /device:TPU:0, one launch (start us, length us, event | category | flops | bytes accessed | tf_op | source)
XLA Modules:
  0.0 206.1 jit_solution(3456944928402386581)
XLA Ops:
  6.5 2.2 %slice_bitcast_fusion.3 = (bf16[1,128,3,1024]{3,1,2,0:T(8,128)(2,1)S(1)}, bf16[1,128,3,1024]{3,1,2,0:T(8,128)(2,1)S(1)}, bf16[1,128,3,1024]{3,1,2,0:T(8,128)(2,1)S(1)}, bf16[1,128,3,1024]{3,1,2,0:T(8,128)(2,1)S(1)}) fusion(bf16[128,3,4096]{2,0,1:T(8,128)(2,1)} %bitcast.232), kind=kLoop, calls=%fused_computation.159 | loop fusion | bytes 6291456 | tf_op jit(solution)/shard_map/stack | solution.py:15
  8.7 1.9 pad_maximum_fusion
  10.6 4.3 %all-to-all-start = ((bf16[4,128,3,1024]{3,1,2,0:T(8,128)(2,1)}), bf16[4,128,3,1024]{3,1,2,0:T(8,128)(2,1)S(1)}, u32[]{:S(2)}, u32[]{:S(2)}) async-start(bf16[4,128,3,1024]{3,1,2,0:T(8,128)(2,1)} %pad_maximum_fusion), calls=%async_computation | async-start | bytes 6291456 | tf_op jit(solution)/shard_map/all_to_all | solution.py:16
  15.7 36.2 %all-to-all-done = bf16[4,128,3,1024]{3,1,2,0:T(8,128)(2,1)S(1)} async-done(((bf16[4,128,3,1024]{3,1,2,0:T(8,128)(2,1)}), bf16[4,128,3,1024]{3,1,2,0:T(8,128)(2,1)S(1)}, u32[]{:S(2)}, u32[]{:S(2)}) %all-to-all-start) | async-done | bytes 3145760 | tf_op jit(solution)/shard_map/all_to_all | solution.py:16
  52.2 0.9 pad_convert_fusion
  53.2 1.9 fusion.123
  55.1 2.7 %copy-done = f32[512,3,1024]{2,0,1:T(8,128)} copy-done((f32[512,3,1024]{2,0,1:T(8,128)}, f32[512,3,1024]{2,0,1:T(8,128)S(1)}, u32[]{:S(2)}) %copy-start) | copy-done | bytes 6291480
  57.7 1.3 fusion.128
  59.0 1.6 all-gather.2.cloned.1.call-done
  60.9 115.5 %while.15 = (s32[]{:T(128)}, f32[512,1024]{1,0:T(8,128)S(1)}, bf16[512,1024]{1,0:T(8,128)(2,1)}, f32[16,16]{1,0:T(8,128)S(1)}, f32[16,16]{1,0:T(8,128)S(1)}, /*i...) while((s32[]{:T(128)}, f32[512,1024]{1,0:T(8,128)S(1)}, ...), condition=%wide.region_1.2_spmd.clone.clone, body=%wide.region_0.1_spmd.clone.clone.sunk | while | flops 1288484864 | bytes 33853592 | solution.py:132
  61.1 1.0 constant_dynamic-slice_fusion.3
  65.4 0.8 convolution_subtract_fusion.6
  66.9 0.8 convolution_add_fusion.6
  70.0 0.9 multiply_add_fusion.4
  73.1 0.9 multiply_add_fusion.5
  75.5 1.0 constant_dynamic-slice_fusion.3
  79.8 0.8 convolution_subtract_fusion.6
  84.4 0.9 multiply_add_fusion.4
  87.5 0.9 multiply_add_fusion.5
  89.9 1.0 constant_dynamic-slice_fusion.3
  94.2 0.8 convolution_subtract_fusion.6
  98.8 0.9 multiply_add_fusion.4
  101.9 0.9 multiply_add_fusion.5
  104.4 1.0 constant_dynamic-slice_fusion.3
  108.7 0.8 convolution_subtract_fusion.6
  111.7 0.8 convolution_add_fusion.5
  113.2 0.9 multiply_add_fusion.4
  116.4 0.9 multiply_add_fusion.5
  118.8 1.0 constant_dynamic-slice_fusion.3
  123.1 0.8 convolution_subtract_fusion.6
  126.1 0.8 convolution_add_fusion.5
  127.6 0.9 multiply_add_fusion.4
  130.8 0.9 multiply_add_fusion.5
  133.2 1.0 constant_dynamic-slice_fusion.3
  137.5 0.8 convolution_subtract_fusion.6
  142.1 0.9 multiply_add_fusion.4
  145.2 0.9 multiply_add_fusion.5
  147.6 1.0 constant_dynamic-slice_fusion.3
  151.9 0.8 convolution_subtract_fusion.6
  156.5 0.9 multiply_add_fusion.4
  159.6 0.9 multiply_add_fusion.5
  162.0 1.0 constant_dynamic-slice_fusion.3
  166.3 0.8 convolution_subtract_fusion.6
  170.9 0.9 multiply_add_fusion.4
  174.0 0.9 multiply_add_fusion.5
  176.5 3.8 %fusion.126 = bf16[512,1024]{1,0:T(8,128)(2,1)S(1)} fusion(f32[512,1024]{1,0:T(8,128)S(1)} %get-tuple-element.246, f32[512,3,1024]{2,0,1:T(8,128)} %copy-done, f32[1024]{0:T(1024)S(1)} %copy-done.2), kind=kLoop, calls=%fused_computation.152 | loop fusion | flops 5242880 | bytes 8392704 | tf_op jit(solution)/shard_map/convert_element_type | solution.py:143
  180.3 17.0 %all_to_all.21 = bf16[4,128,1024]{2,1,0:T(8,128)(2,1)S(1)} all-to-all(bf16[4,128,1024]{2,1,0:T(8,128)(2,1)S(1)} %bitcast.231), channel_id=1, replica_groups=mesh['dp'=8,'ctx'=4] {'ctx'}, dimensions={0} | all-to-all | bytes 2097152 | tf_op jit(solution)/shard_map/all_to_all | solution.py:154
  198.0 1.3 copy.34
  (209 shorter events, 84.8 us)
Async XLA Ops:
  10.5 5.1 %copy-start.1 = (f32[3,3,1024]{2,1,0:T(4,128)S(1)}, f32[3,3,1024]{2,1,0:T(4,128)}, u32[]{:S(2)}) copy-start(f32[3,3,1024]{2,1,0:T(4,128)} %param.7) | copy-start | bytes 110596
  10.6 41.3 %all-to-all-start = ((bf16[4,128,3,1024]{3,1,2,0:T(8,128)(2,1)}), bf16[4,128,3,1024]{3,1,2,0:T(8,128)(2,1)S(1)}, u32[]{:S(2)}, u32[]{:S(2)}) async-start(bf16[4,128,3,1024]{3,1,2,0:T(8,128)(2,1)} %pad_maximum_fusion), calls=%async_computation | async-start | bytes 6291456 | tf_op jit(solution)/shard_map/all_to_all | solution.py:16
  14.9 45.8 %all-gather.2.cloned.1.call-start = ((), (), s32[]{:S(2)}) async-start(), calls=%async_computation.2 | async-start | bytes 1179648 | tf_op jit(solution)/shard_map/all_gather | solution.py:149
  55.1 2.7 %copy-start = (f32[512,3,1024]{2,0,1:T(8,128)}, f32[512,3,1024]{2,0,1:T(8,128)S(1)}, u32[]{:S(2)}) copy-start(f32[512,3,1024]{2,0,1:T(8,128)S(1)} %fusion.123) | copy-start | bytes 18874372
  60.9 115.5 %copy-start.2 = (f32[1024]{0:T(1024)S(1)}, f32[1024]{0:T(1024)}, u32[]{:S(2)}) copy-start(f32[1024]{0:T(1024)} %param.9) | copy-start | bytes 12292
Sparse Core Ops, SparseCore 0:
  17.8 42.7 all-gather.1
